TPU v7x, 32 devices: a whole 2x2x4 slice. The times are simulated.
32 devices in a mesh: ctx: 8 (over y, x, core), mp: 4 (over z).
Axes of the slice: x: 2, y: 2, z: 4, core: 2. Of those that a mesh axis runs over, the one named last changes fastest.
Arguments:
- resid_in: bfloat16 [4096, 8192], P('ctx', 'mp'), may hold values from -6 to 6
- q_mr: bfloat16 [4096, 8192], P('ctx', 'mp'), may hold values from -6 to 6
- k_mr: bfloat16 [4096, 8192], P('ctx', 'mp'), may hold values from -6 to 6
- v_mr: bfloat16 [4096, 8192], P('ctx', 'mp'), may hold values from -6 to 6
- mr_filter: float32 [128, 8192], P(None, 'mp'), may hold values from -0.5 to 0.5
- mr_out: bfloat16 [8192, 8192], P('ctx', 'mp'), may hold values from -0.0625 to 0.0625
- q_li: bfloat16 [4096, 8192], P('ctx', 'mp'), may hold values from -6 to 6
- k_li: bfloat16 [4096, 8192], P('ctx', 'mp'), may hold values from -6 to 6
- li_rate: float32 [8192], P('mp'), may hold values from 2.4414063e-05 to 0.0333333333
- li_residue: float32 [8192], P('mp'), may hold values from 0.5 to 2
Outputs:
- mixed: bfloat16 [4096, 8192], P('ctx', 'mp')
- long_out: bfloat16 [4096, 8192], P('ctx', 'mp')
All inputs are finite; a program needn't handle non-finite values.
Results may differ from a plain program's by a relative error of at most 0.008.
Values may be sent and summed in bfloat16 or wider, within the bound.
A program may use at most 192 MiB of HBM per device.

v0:
```python
import jax
import jax.numpy as jnp
from jax import lax
from jax.sharding import PartitionSpec as P


def passed_along(value, axis, by):
    peers = lax.axis_size(axis)
    pairs = [(i, i + by) for i in range(peers) if 0 <= i + by < peers]
    return lax.ppermute(value, axis, pairs)


def carried_in(value, axis, join, neutral):
    count, mine = (lax.axis_size(axis), lax.axis_index(axis))
    pieces = jax.tree.map(lambda part: lax.all_gather(part, axis), value)
    subtotal = jax.tree.map(
        lambda part, zero: jnp.full_like(part, 0) + jnp.asarray(zero, part.dtype), value, neutral
    )

    def step(position, subtotal):
        longer = join(subtotal, jax.tree.map(lambda part: part[position], pieces))
        return jax.tree.map(lambda new, old: jnp.where(position < mine, new, old), longer, subtotal)

    return lax.fori_loop(0, count - 1, step, subtotal)


def link_pair(earlier, later):
    return (earlier[0] * later[0], later[0] * earlier[1] + later[1])


def body(resid_in, q_mr, k_mr, v_mr, mr_filter, mr_out, q_li, k_li, li_rate, li_residue):
    row_count = q_mr.shape[0]
    chan_count = q_mr.shape[1]
    tap_count = mr_filter.shape[0]
    drive_mr = (k_mr.astype(jnp.float32) * v_mr.astype(jnp.float32)).astype(jnp.bfloat16)
    prev_rows = passed_along(drive_mr[row_count - (tap_count - 1) :], "ctx", 1)
    padded = jnp.concatenate([prev_rows, drive_mr], 0).astype(jnp.float32)[None]
    kernel = mr_filter[::-1][:, None, :]
    filtered = lax.conv_general_dilated(
        padded,
        kernel,
        (1,),
        "VALID",
        dimension_numbers=("NWC", "WIO", "NWC"),
        feature_group_count=chan_count,
        precision=lax.Precision.HIGHEST,
    )[0]
    gated = (q_mr.astype(jnp.float32) * filtered).astype(jnp.bfloat16)
    gathered = lax.all_gather(gated, "mp", axis=1, tiled=True)
    all_rows = lax.all_gather(mr_out, "ctx", axis=0, tiled=True)
    summed = jnp.dot(gathered, all_rows, preferred_element_type=jnp.float32)
    mixed = (resid_in.astype(jnp.float32) + summed).astype(jnp.bfloat16)
    decay = jnp.exp(-li_rate)
    drive_li = k_li.astype(jnp.float32) * mixed.astype(jnp.float32)
    decay_rows = jnp.broadcast_to(decay[None, :], drive_li.shape)
    _, local_state = lax.associative_scan(link_pair, (decay_rows, drive_li), axis=0)
    offsets = jnp.arange(1, row_count + 1, dtype=jnp.float32)[:, None]
    powers = jnp.exp(-li_rate[None, :] * offsets)
    block_end = local_state[row_count - 1]
    block_decay = jnp.exp(-li_rate * row_count)
    identity = (jnp.ones_like(block_decay), jnp.zeros_like(block_end))
    prefix = carried_in((block_decay, block_end), "ctx", link_pair, identity)
    carried = prefix[1]
    state = local_state + powers * carried[None, :]
    scale = li_residue * jnp.sqrt(-jnp.expm1(-2.0 * li_rate))
    long_out = (q_li.astype(jnp.float32) * scale * state).astype(jnp.bfloat16)
    return (mixed, long_out)


def solution(mesh):
    in_specs = (
        P("ctx", "mp"),
        P("ctx", "mp"),
        P("ctx", "mp"),
        P("ctx", "mp"),
        P(None, "mp"),
        P("ctx", "mp"),
        P("ctx", "mp"),
        P("ctx", "mp"),
        P("mp"),
        P("mp"),
    )
    out_specs = (P("ctx", "mp"), P("ctx", "mp"))
    return jax.shard_map(body, mesh=mesh, in_specs=in_specs, out_specs=out_specs, check_vma=False)
```

profile of v0, /device:TPU:0, one launch (start us, length us, event | category | flops | bytes accessed | tf_op | source)
XLA Modules:
  0.0 563.9 jit_solution(2799196935869276048)
XLA Ops:
  7.2 3.1 multiply_convert_fusion.1
  10.3 0.9 slice.256
  11.2 3.2 collective-permute-start
  14.4 5.2 rev.3
  19.6 1.8 maximum_bitcast_fusion
  21.4 45.6 %fusion = f32[1,512,2048]{2,0,1:T(1,128)S(1)} fusion(bf16[1,639,2048]{2,1,0:T(8,128)(2,1)S(1)} %maximum_bitcast_fusion, f32[128,1,2048]{2,0,1:T(8,128)S(1)} %bitcast.22), kind=kOutput, calls=%fused_computation.3 | convolution fusion | flops 1610612736 | bytes 7860224 | tf_op jit(solution)/shard_map/conv_general_dilated | solution.py:39
  67.0 2.9 fusion.2
  71.4 14.1 %all-gather = f32[16384]{0:T(1024)S(1)} all-gather(f32[2048]{0:T(1024)S(1)} %get-tuple-element.139), channel_id=2, replica_groups=mesh['ctx'=8,'mp'=4] {'ctx'}, dimensions={0}, use_global_device_ids=true | all-gather | bytes 73728 | tf_op jit(solution)/shard_map/all_gather | solution.py:15
  86.8 138.0 %all-gather.5.cloned.1.call-done = bf16[512,8192]{1,0:T(8,128)(2,1)} async-done(((bf16[512,2048]{1,0:T(8,128)(2,1)}), bf16[512,8192]{1,0:T(8,128)(2,1)}) %all-gather.5.cloned.1.call-update) | async-done | bytes 8388624 | tf_op jit(solution)/shard_map/all_gather | solution.py:49
  224.8 160.9 %all-gather.7.cloned.1.call-done = bf16[8192,2048]{1,0:T(8,128)(2,1)} async-done(((bf16[1024,2048]{1,0:T(8,128)(2,1)}), bf16[8192,2048]{1,0:T(8,128)(2,1)}) %all-gather.7.cloned.1.call-update) | async-done | bytes 33554448 | tf_op jit(solution)/shard_map/all_gather | solution.py:50
  385.6 25.6 %convert_multiply_fusion = (f32[512,2048]{1,0:T(8,128)}, bf16[512,2048]{1,0:T(8,128)(2,1)}) fusion(bf16[512,2048]{1,0:T(8,128)(2,1)} %param.19, bf16[512,8192]{1,0:T(8,128)(2,1)} %all-gather.5.cloned.1.call-done, bf16[8192,2048]{1,0:T(8,128)(2,1)} %all-gather.7.cloned.1.call-done, bf16[512,2048]{1,0:T(8,128)(2,1)} %param.12), kind=kOutput, calls=%fused_computation.8 | convolution fusion | flops 17186160640 | bytes 52428800 | tf_op jit(solution)/shard_map/dot_general | solution.py:51
  411.3 10.0 %slice.254 = f32[255,2048]{1,0:T(8,128)} slice(f32[512,2048]{1,0:T(8,128)} %get-tuple-element.143), slice={[2:512:2], [0:2048:1]} | slice | bytes 4177920 | tf_op jit(solution)/shard_map/slice | solution.py:56
  421.3 9.8 %slice.200 = f32[256,2048]{1,0:T(8,128)} slice(f32[512,2048]{1,0:T(8,128)} %get-tuple-element.143), slice={[1:512:2], [0:2048:1]} | slice | bytes 4194304 | tf_op jit(solution)/shard_map/slice | solution.py:56
  431.1 9.8 %slice.199 = f32[256,2048]{1,0:T(8,128)} slice(f32[512,2048]{1,0:T(8,128)} %get-tuple-element.143), slice={[0:511:2], [0:2048:1]} | slice | bytes 4194304 | tf_op jit(solution)/shard_map/slice | solution.py:56
  440.9 2.6 multiply_add_fusion
  443.5 2.9 slice.205
  446.4 2.8 slice.204
  449.3 1.7 multiply_add_fusion.1
  450.9 1.7 slice.250
  452.7 1.5 slice.210
  454.1 1.5 slice.209
  455.6 2.1 multiply_add_fusion.2
  457.7 1.7 slice.215
  459.4 1.7 slice.214
  461.1 1.1 multiply_add_fusion.3
  464.2 1.0 multiply_add_fusion.4
  466.5 1.5 multiply_add_fusion.5
  468.0 1.5 slice.242
  469.5 1.5 slice.230
  471.0 1.4 slice.229
  472.4 1.4 multiply_add_fusion.6
  473.8 1.4 slice.235
  475.2 1.4 slice.234
  478.4 1.1 slice.248
  479.6 3.0 slice.252
  482.6 1.4 slice.257
  489.3 0.9 copy-done.2
  490.2 1.1 add.181
  491.3 4.2 pad.70
  495.6 1.8 fusion.4
  497.4 4.9 pad.69
  502.3 3.4 add.183
  506.4 1.5 pad_maximum_fusion
  507.9 16.7 %pad.71 = f32[512,2048]{1,0:T(8,128)} pad(f32[256,2048]{1,0:T(8,128)} %pad_maximum_fusion, f32[]{:T(128)} %constant.35.clone.1), padding=0_1_1x0_0_0 | pad | bytes 6291460 | tf_op jit(solution)/shard_map/pad | solution.py:56
  524.7 9.1 %pad.72 = f32[512,2048]{1,0:T(8,128)} pad(f32[256,2048]{1,0:T(8,128)S(1)} %copy-done.3, f32[]{:T(128)} %constant.35.clone.1), padding=1_0_1x0_0_0 | pad | bytes 6291460 | tf_op jit(solution)/shard_map/pad | solution.py:56
  534.6 9.2 %all-gather.1 = f32[8,1,2048]{2,1,0:T(1,128)S(1)} all-gather(f32[1,1,2048]{2,1,0:T(1,128)S(1)} %add_bitcast_fusion), channel_id=1, replica_groups=mesh['ctx'=8,'mp'=4] {'ctx'}, dimensions={0}, use_global_device_ids=true | all-gather | bytes 73728 | tf_op jit(solution)/shard_map/all_gather | solution.py:15
  543.8 6.3 %while.14 = (s32[]{:T(128)}, f32[2048]{0:T(1024)S(1)}, s32[]{:T(128)}, f32[8,2048]{1,0:T(8,128)}, f32[8,2048]{1,0:T(8,128)S(1)}, /*index=5*/s32[]{:T(128)}, s32[]{:T(128)}) while((s32[]{:T(128)}, f32[2048]{0:T(1024)S(1)}, s32[]{:T(128)}, f32[8,2048]{1,0:T(8,128)}, f32[8,2048]{1,0:T(8,128)S(1)}, /*index=5*/s32[]{:T(128)}, ...), condition=%wide.region_1.2_spmd.clone, body=%wide.region_0.1_spmd.clone.sunk | while | flops 8196 | bytes 65645 | solution.py:24
  550.2 6.9 %multiply_convert_fusion = bf16[512,2048]{1,0:T(8,128)(2,1)} fusion(f32[512,2048]{1,0:T(8,128)} %pad.71, f32[512,2048]{1,0:T(8,128)} %pad.72, bf16[512,2048]{1,0:T(8,128)(2,1)} %param.18, f32[2048]{0:T(1024)S(1)} %get-tuple-element.96, f32[512]{0:T(512)S(1)} %copy-done.28, f32[2048]{0:T(1024)S(1)} %copy-done.24, f32[2048]{0:T(1024)S(1)} %copy-done.23), kind=kLoop, calls=%fused_computation.7 | loop fusion | flops 8388608 | bytes 12609536 | tf_op jit(solution)/shard_map/convert_element_type | solution.py:66
  (136 shorter events, 20.7 us)
Async XLA Ops:
  7.2 7.2 %copy-start.8 = (f32[128,2048]{1,0:T(8,128)S(1)}, f32[128,2048]{1,0:T(8,128)}, u32[]{:S(2)}) copy-start(f32[128,2048]{1,0:T(8,128)} %param.16) | copy-start | bytes 3145732
  7.2 217.6 %all-gather.5.cloned.1.call-start = ((), (), s32[]{:S(2)}) async-start(), calls=%async_computation | async-start | bytes 10485760 | tf_op jit(solution)/shard_map/all_gather | solution.py:49
  11.2 8.3 %collective-permute-start = (bf16[127,2048]{1,0:T(8,128)(2,1)}, bf16[127,2048]{1,0:T(8,128)(2,1)}, u32[]{:S(2)}, u32[]{:S(2)}) collective-permute-start(bf16[127,2048]{1,0:T(8,128)(2,1)} %slice.256), channel_id=1, source_target_pairs={{0,4},{4,8},{8,12},{12,16},{16,20},{20,24},{24,28},{1,5},{5,9},{9,... | collective-permute-start | bytes 1560584 | tf_op jit(solution)/shard_map/ppermute | solution.py:10
  19.6 1.8 copy-start.9
  21.4 45.6 %copy-start.7 = (bf16[512,2048]{1,0:T(8,128)(2,1)S(1)}, bf16[512,2048]{1,0:T(8,128)(2,1)}, u32[]{:S(2)}) copy-start(bf16[512,2048]{1,0:T(8,128)(2,1)} %param.13) | copy-start | bytes 6291460
  69.9 0.8 copy-start.29
  69.9 0.8 copy-start.30
  69.9 315.7 %all-gather.7.cloned.1.call-start = ((), (), s32[]{:S(2)}) async-start(), calls=%async_computation.1 | async-start | bytes 37748736 | tf_op jit(solution)/shard_map/all_gather | solution.py:50
  71.3 369.6 %copy-start.12 = (f32[2048]{0:T(1024)}, f32[2048]{0:T(1024)S(1)}, u32[]{:S(2)}) copy-start(f32[2048]{0:T(1024)S(1)} %get-tuple-element.138) | copy-start | bytes 24580
  71.3 377.9 %copy-start.14 = (f32[2048]{0:T(1024)}, f32[2048]{0:T(1024)S(1)}, u32[]{:S(2)}) copy-start(f32[2048]{0:T(1024)S(1)} %get-tuple-element.141) | copy-start | bytes 24580
  71.3 384.2 %copy-start.16 = (f32[2048]{0:T(1024)}, f32[2048]{0:T(1024)S(1)}, u32[]{:S(2)}) copy-start(f32[2048]{0:T(1024)S(1)} %get-tuple-element.140) | copy-start | bytes 24580
  71.3 389.7 %copy-start.18 = (f32[2048]{0:T(1024)}, f32[2048]{0:T(1024)S(1)}, u32[]{:S(2)}) copy-start(f32[2048]{0:T(1024)S(1)} %get-tuple-element.132) | copy-start | bytes 24580
  71.4 392.9 %copy-start.20 = (f32[2048]{0:T(1024)}, f32[2048]{0:T(1024)S(1)}, u32[]{:S(2)}) copy-start(f32[2048]{0:T(1024)S(1)} %get-tuple-element.133) | copy-start | bytes 24580
  443.5 39.1 %copy-start.1 = (f32[256,2048]{1,0:T(8,128)}, f32[256,2048]{1,0:T(8,128)S(1)}, u32[]{:S(2)}) copy-start(f32[256,2048]{1,0:T(8,128)S(1)} %multiply_add_fusion) | copy-start | bytes 6291460
  450.9 28.6 %copy-start.5 = (f32[128,2048]{1,0:T(8,128)}, f32[128,2048]{1,0:T(8,128)S(1)}, u32[]{:S(2)}) copy-start(f32[128,2048]{1,0:T(8,128)S(1)} %multiply_add_fusion.1) | copy-start | bytes 3145732
  468.0 19.3 %slice-start.3 = ((f32[8,2048]{1,0:T(8,128)}), f32[1,2048]{1,0:T(1,128)S(1)}, s32[]{:S(2)}) async-start(f32[8,2048]{1,0:T(8,128)} %multiply_add_fusion.5), calls=%async_computation.5 | async-start | bytes 16384 | tf_op jit(solution)/shard_map/slice | solution.py:56
  477.8 9.8 %copy-start.10 = (f32[15,2048]{1,0:T(8,128)S(1)}, f32[15,2048]{1,0:T(8,128)}, u32[]{:S(2)}) copy-start(f32[15,2048]{1,0:T(8,128)} %slice.246) | copy-start | bytes 368644
  479.5 7.9 %copy-start.11 = (f32[7,2048]{1,0:T(8,128)S(1)}, f32[7,2048]{1,0:T(8,128)}, u32[]{:S(2)}) copy-start(f32[7,2048]{1,0:T(8,128)} %slice.244) | copy-start | bytes 172036
  479.6 7.9 %copy-start.22 = (f32[2048]{0:T(1024)S(1)}, f32[2048]{0:T(1024)}, u32[]{:S(2)}) copy-start(f32[2048]{0:T(1024)} %get-tuple-element.135) | copy-start | bytes 24580
  479.6 7.9 %copy-start.27 = (f32[1,2048]{1,0:T(1,128)S(1)}, f32[1,2048]{1,0:T(1,128)}, u32[]{:S(2)}) copy-start(f32[1,2048]{1,0:T(1,128)} %slice.262) | copy-start | bytes 24580
  479.6 8.0 %copy-start.21 = (f32[2048]{0:T(1024)S(1)}, f32[2048]{0:T(1024)}, u32[]{:S(2)}) copy-start(f32[2048]{0:T(1024)} %copy-done.20) | copy-start | bytes 24580
  479.6 8.0 %copy-start.26 = (f32[1,2048]{1,0:T(1,128)S(1)}, f32[1,2048]{1,0:T(1,128)}, u32[]{:S(2)}) copy-start(f32[1,2048]{1,0:T(1,128)} %slice.261) | copy-start | bytes 24580
  485.5 2.4 copy-start.19
  487.4 0.7 slice-start.2
  487.7 1.0 copy-start.6
  487.8 1.0 copy-start.17
  488.1 0.7 slice-start.1
  489.2 1.0 copy-start.2
  490.2 5.3 copy-start.15
  495.5 1.8 slice-start
  502.3 3.4 copy-start
  502.3 3.4 copy-start.4
  502.3 3.4 copy-start.13
  505.7 0.7 copy-start.25
  507.9 16.7 %copy-start.3 = (f32[256,2048]{1,0:T(8,128)S(1)}, f32[256,2048]{1,0:T(8,128)}, u32[]{:S(2)}) copy-start(f32[256,2048]{1,0:T(8,128)} %add.183) | copy-start | bytes 6291460
  524.6 25.5 %copy-start.23 = (f32[2048]{0:T(1024)S(1)}, f32[2048]{0:T(1024)}, u32[]{:S(2)}) copy-start(f32[2048]{0:T(1024)} %get-tuple-element.131) | copy-start | bytes 24580
  524.7 25.5 %copy-start.24 = (f32[2048]{0:T(1024)S(1)}, f32[2048]{0:T(1024)}, u32[]{:S(2)}) copy-start(f32[2048]{0:T(1024)} %get-tuple-element.142) | copy-start | bytes 24580
  524.7 25.5 %copy-start.28 = (f32[512]{0:T(512)S(1)}, f32[512]{0:T(512)}, u32[]{:S(2)}) copy-start(f32[512]{0:T(512)} %iota_add_fusion) | copy-start | bytes 6148
Sparse Core Ops, SparseCore 0:
  70.0 154.7 all-gather.4
  226.6 158.9 all-gather.6
where the time goes:
time: 566 us; the launch traced here: 564 us
  waiting for transfers between devices  300 us (53%)
  local copies, waits for them, and re-layouts  111 us (20%)
  matrix products  71.2 us (13%)
  other arithmetic  40.3 us (7%)
  blocking collectives  23.3 us (4%)
  between operations  14.7 us (3%)
    all_gather x1, waiting for transfers between devices, body(): all_rows = lax.all_gather(mr_out, 'ctx', axis=0, tiled=True)  161 us
    all_gather x1, waiting for transfers between devices, body(): gathered = lax.all_gather(gated, 'mp', axis=1, tiled=True)  138 us
    slice x34, local copies, waits for them, and re-layouts, body(): lax.associative_scan(link_pair, (decay_rows, drive_li), axis=0)  61.5 us
    conv_general_dilated x1, matrix products, body(): lax.conv_general_dilated(padded, kernel, (1,), 'VALID', dimension_numbers...  45.6 us
    pad x16, local copies, waits for them, and re-layouts, body(): lax.associative_scan(link_pair, (decay_rows, drive_li), axis=0)  35.5 us
    dot_general x1, matrix products, body(): summed = jnp.dot(gathered, all_rows, preferred_element_type=jnp.float32)  25.6 us
    all_gather x2, blocking collectives, carried_in(): pieces = jax.tree.map(lambda part: lax.all_gather(part, axis), value)  23.3 us
    add x16, other arithmetic, link_pair(): return (earlier[0] * later[0], later[0] * earlier[1] + later[1])  16.2 us
  transfers between devices with their start and end apart: 3, of which 2 were waited for; matrix products, arithmetic and copies ran while one was open for 1% of the time, Pallas kernels for 0%

commit v1 on v0

--- a/solution.py
+++ b/solution.py
@@ -46,7 +46,12 @@
         precision=lax.Precision.HIGHEST,
     )[0]
     gated = (q_mr.astype(jnp.float32) * filtered).astype(jnp.bfloat16)
-    gathered = lax.all_gather(gated, "mp", axis=1, tiled=True)
+    ring = [gated]
+    for hop in range(3):
+        ring.append(lax.ppermute(ring[-1], "mp", [(dev, (dev + 1) % 4) for dev in range(4)]))
+    gathered = jnp.roll(
+        jnp.concatenate(ring[::-1], axis=1), (lax.axis_index("mp") + 1) * ring[0].shape[1], axis=1
+    )
     all_rows = lax.all_gather(mr_out, "ctx", axis=0, tiled=True)
     summed = jnp.dot(gathered, all_rows, preferred_element_type=jnp.float32)
     mixed = (resid_in.astype(jnp.float32) + summed).astype(jnp.bfloat16)

time: 566 us -> 414 us (0.73)
  waiting for transfers between devices: 300 us -> 136 us
  local copies, waits for them, and re-layouts: 111 us -> 129 us
  blocking collectives: 23.3 us -> 17.2 us
    all_gather x1, waiting for transfers between devices: 161 us -> 0.01 us  [body(): all_rows = lax.all_gather(mr_out, 'ctx', axis=0, tiled=True)]
    all_gather x1 -> x0, waiting for transfers between devices: 138 us -> none  [body(): gathered = lax.all_gather(gated, 'mp', axis=1, tiled=True)]
    ppermute x0 -> x3, waiting for transfers between devices: none -> 136 us  [body(): lax.ppermute(ring[-1], 'mp', [(dev, (dev + 1) % 4) for dev in range(4)])]
    unnamed x63 -> x78, local copies, waits for them, and re-layouts: 1.57 us -> 18.8 us
    all_gather x2, blocking collectives: 23.3 us -> 17.2 us  [carried_in(): pieces = jax.tree.map(lambda part: lax.all_gather(part, axis), value)]
  transfers between devices with their start and end apart: 3 -> 5, of which waited for: 2 -> 3; matrix products, arithmetic and copies ran while one was open for 1% -> 19% of each run, Pallas kernels for 0% -> 0%
where the time goes in v1:
time: 414 us; the launch traced here: 412 us
  waiting for transfers between devices  136 us (33%)
  local copies, waits for them, and re-layouts  129 us (31%)
  matrix products  71.3 us (17%)
  other arithmetic  37.2 us (9%)
  blocking collectives  17.2 us (4%)
  between operations  14.8 us (4%)
  starting transfers between devices  5.91 us (1%)
    ppermute x3, waiting for transfers between devices, body(): lax.ppermute(ring[-1], 'mp', [(dev, (dev + 1) % 4) for dev in range(4)])  136 us
    slice x34, local copies, waits for them, and re-layouts, body(): lax.associative_scan(link_pair, (decay_rows, drive_li), axis=0)  61 us
    conv_general_dilated x1, matrix products, body(): lax.conv_general_dilated(padded, kernel, (1,), 'VALID', dimension_numbers...  45.6 us
    pad x16, local copies, waits for them, and re-layouts, body(): lax.associative_scan(link_pair, (decay_rows, drive_li), axis=0)  35.2 us
    dot_general x1, matrix products, body(): summed = jnp.dot(gathered, all_rows, preferred_element_type=jnp.float32)  25.7 us
    unnamed x78, local copies, waits for them, and re-layouts  18.8 us
    all_gather x2, blocking collectives, carried_in(): pieces = jax.tree.map(lambda part: lax.all_gather(part, axis), value)  17.2 us
    add x16, other arithmetic, link_pair(): return (earlier[0] * later[0], later[0] * earlier[1] + later[1])  15.7 us
  transfers between devices with their start and end apart: 5, of which 3 were waited for; matrix products, arithmetic and copies ran while one was open for 19% of the time, Pallas kernels for 0%

profile of v1, /device:TPU:0, one launch (start us, length us, event | category | flops | bytes accessed | tf_op | source)
XLA Modules:
  0.0 412.0 jit_solution(18292344556680172116)
XLA Ops:
  7.9 3.1 multiply_convert_fusion.1
  11.9 3.2 collective-permute-start
  15.1 5.2 %rev.3 = f32[128,2048]{1,0:T(8,128)} reverse(f32[128,2048]{1,0:T(8,128)S(1)} %copy-done.6), dimensions={0} | reverse | bytes 2097152 | tf_op jit(solution)/shard_map/rev | solution.py:38
  20.3 1.9 maximum_bitcast_fusion
  22.2 45.6 %fusion.2 = f32[1,512,2048]{2,0,1:T(1,128)S(1)} fusion(bf16[1,639,2048]{2,1,0:T(8,128)(2,1)S(1)} %maximum_bitcast_fusion, f32[128,1,2048]{2,0,1:T(8,128)S(1)} %bitcast.21), kind=kOutput, calls=%fused_computation.5 | convolution fusion | flops 1610612736 | bytes 7860224 | tf_op jit(solution)/shard_map/conv_general_dilated | solution.py:39
  67.8 2.3 fusion.4
  70.2 2.5 collective-permute-start.1
  72.7 47.2 %collective-permute-done.1 = bf16[512,2048]{1,0:T(8,128)(2,1)S(1)} collective-permute-done((bf16[512,2048]{1,0:T(8,128)(2,1)S(1)}, bf16[512,2048]{1,0:T(8,128)(2,1)S(1)}, u32[]{:S(2)}, u32[]{:S(2)}) %collective-permute-start.1) | collective-permute-done | bytes 2097184 | tf_op jit(solution)/shard_map/ppermute | solution.py:51
  121.4 50.0 %collective-permute-done.2 = bf16[512,2048]{1,0:T(8,128)(2,1)} collective-permute-done((bf16[512,2048]{1,0:T(8,128)(2,1)S(1)}, bf16[512,2048]{1,0:T(8,128)(2,1)}, u32[]{:S(2)}, u32[]{:S(2)}) %collective-permute-start.2) | collective-permute-done | bytes 2097184 | tf_op jit(solution)/shard_map/ppermute | solution.py:51
  172.1 9.4 %all-gather = f32[16384]{0:T(1024)S(1)} all-gather(f32[2048]{0:T(1024)S(1)} %get-tuple-element.139), channel_id=2, replica_groups=mesh['ctx'=8,'mp'=4] {'ctx'}, dimensions={0}, use_global_device_ids=true | all-gather | bytes 73728 | tf_op jit(solution)/shard_map/all_gather | solution.py:15
  182.8 38.4 %collective-permute-done.3 = bf16[512,2048]{1,0:T(8,128)(2,1)} collective-permute-done((bf16[512,2048]{1,0:T(8,128)(2,1)}, bf16[512,2048]{1,0:T(8,128)(2,1)}, u32[]{:S(2)}, u32[]{:S(2)}) %collective-permute-start.3) | collective-permute-done | bytes 2097184 | tf_op jit(solution)/shard_map/ppermute | solution.py:51
  221.2 3.1 constant_dynamic-update-slice_fusion.7
  224.3 3.1 constant_dynamic-update-slice_fusion.6
  227.5 1.4 constant_dynamic-update-slice_fusion.5
  228.9 1.4 constant_dynamic-update-slice_fusion.4
  230.3 3.1 constant_dynamic-update-slice_fusion.3
  233.4 3.1 constant_dynamic-update-slice_fusion.2
  237.9 1.4 constant_dynamic-update-slice_fusion
  239.3 25.7 %convert_multiply_fusion = (f32[512,2048]{1,0:T(8,128)}, bf16[512,2048]{1,0:T(8,128)(2,1)}) fusion(bf16[512,2048]{1,0:T(8,128)(2,1)} %param.19, bf16[8192,2048]{1,0:T(8,128)(2,1)} %all-gather.4.cloned.1.call-done, bf16[512,16384]{1,0:T(8,128)(2,1)} %constant_dynamic-update-slice_fusion, s32[]{:T(128)S(6)} %select_n.36, bf16[512,2048]{1,0:T(8,128)(2,1)} %param.12), kind=kOutput, calls=%fused_computation.10 | convolution fusion | flops 17186160640 | bytes 52428804 | tf_op jit(solution)/shard_map/dot_general | solution.py:56
  265.0 9.8 %slice.199 = f32[256,2048]{1,0:T(8,128)} slice(f32[512,2048]{1,0:T(8,128)} %get-tuple-element.143), slice={[0:511:2], [0:2048:1]} | slice | bytes 4194304 | tf_op jit(solution)/shard_map/slice | solution.py:61
  274.8 9.8 %slice.200 = f32[256,2048]{1,0:T(8,128)} slice(f32[512,2048]{1,0:T(8,128)} %get-tuple-element.143), slice={[1:512:2], [0:2048:1]} | slice | bytes 4194304 | tf_op jit(solution)/shard_map/slice | solution.py:61
  284.6 2.6 multiply_add_fusion
  287.2 3.3 slice.204
  290.5 2.8 slice.205
  293.3 1.7 multiply_add_fusion.1
  295.0 1.6 slice.209
  296.6 1.5 slice.210
  298.0 2.1 multiply_add_fusion.2
  300.1 1.7 slice.214
  301.8 1.7 slice.215
  308.2 1.5 multiply_add_fusion.5
  309.7 1.5 slice.229
  311.2 1.5 slice.230
  316.8 1.5 slice.242
  321.3 1.5 slice.250
  322.9 3.0 slice.252
  325.9 10.1 %slice.254 = f32[255,2048]{1,0:T(8,128)} slice(f32[512,2048]{1,0:T(8,128)} %get-tuple-element.143), slice={[2:512:2], [0:2048:1]} | slice | bytes 4177920 | tf_op jit(solution)/shard_map/slice | solution.py:61
  336.0 1.4 slice.257
  339.8 1.4 fusion.8
  342.4 4.2 %pad.69 = f32[256,2048]{1,0:T(8,128)S(1)} pad(f32[128,2048]{1,0:T(8,128)} %pad_maximum_fusion.1, f32[]{:T(128)} %constant.64.clone.1), padding=0_1_1x0_0_0 | pad | bytes 3145732 | tf_op jit(solution)/shard_map/pad | solution.py:61
  346.6 4.8 %pad.70 = f32[256,2048]{1,0:T(8,128)} pad(f32[128,2048]{1,0:T(8,128)S(1)} %add.197, f32[]{:T(128)} %constant.64.clone.1), padding=1_0_1x0_0_0 | pad | bytes 3145732 | tf_op jit(solution)/shard_map/pad | solution.py:61
  351.4 3.2 add.199
  354.6 16.5 %pad.72 = f32[512,2048]{1,0:T(8,128)} pad(f32[256,2048]{1,0:T(8,128)} %add.199, f32[]{:T(128)} %constant.64.clone.1), padding=1_0_1x0_0_0 | pad | bytes 6291460 | tf_op jit(solution)/shard_map/pad | solution.py:61
  371.1 2.8 fusion.7
  374.2 9.0 %pad.71 = f32[512,2048]{1,0:T(8,128)} pad(f32[256,2048]{1,0:T(8,128)S(1)} %pad_maximum_fusion, f32[]{:T(128)} %constant.64.clone.1), padding=0_1_1x0_0_0 | pad | bytes 6291460 | tf_op jit(solution)/shard_map/pad | solution.py:61
  384.1 7.8 %all-gather.1 = f32[8,1,2048]{2,1,0:T(1,128)S(1)} all-gather(f32[1,1,2048]{2,1,0:T(1,128)S(1)} %add_bitcast_fusion), channel_id=1, replica_groups=mesh['ctx'=8,'mp'=4] {'ctx'}, dimensions={0}, use_global_device_ids=true | all-gather | bytes 73728 | tf_op jit(solution)/shard_map/all_gather | solution.py:15
  391.9 6.3 %while.14 = (s32[]{:T(128)}, f32[2048]{0:T(1024)S(1)}, s32[]{:T(128)}, f32[8,2048]{1,0:T(8,128)}, f32[8,2048]{1,0:T(8,128)S(1)}, /*index=5*/s32[]{:T(128)}, s32[]{:T(128)}) while((s32[]{:T(128)}, f32[2048]{0:T(1024)S(1)}, s32[]{:T(128)}, f32[8,2048]{1,0:T(8,128)}, f32[8,2048]{1,0:T(8,128)S(1)}, /*index=5*/s32[]{:T(128)}, ...), condition=%wide.region_1.2_spmd.clone, body=%wide.region_0.1_spmd.clone.sunk | while | flops 8196 | bytes 65637 | solution.py:24
  398.3 6.9 %multiply_convert_fusion = bf16[512,2048]{1,0:T(8,128)(2,1)} fusion(f32[512,2048]{1,0:T(8,128)} %pad.71, f32[512,2048]{1,0:T(8,128)} %pad.72, bf16[512,2048]{1,0:T(8,128)(2,1)} %param.18, f32[2048]{0:T(1024)S(1)} %get-tuple-element.96, f32[512]{0:T(512)S(1)} %copy-done.32, f32[2048]{0:T(1024)S(1)} %copy-done.27, f32[2048]{0:T(1024)S(1)} %copy-done.26), kind=kLoop, calls=%fused_computation.9 | loop fusion | flops 8388608 | bytes 12609536 | tf_op jit(solution)/shard_map/convert_element_type | solution.py:71
  (155 shorter events, 28.8 us)
Async XLA Ops:
  7.2 232.2 %all-gather.4.cloned.1.call-start = ((), (), s32[]{:S(2)}) async-start(), calls=%async_computation | async-start | bytes 37748736 | tf_op jit(solution)/shard_map/all_gather | solution.py:55
  7.9 7.2 %copy-start.6 = (f32[128,2048]{1,0:T(8,128)S(1)}, f32[128,2048]{1,0:T(8,128)}, u32[]{:S(2)}) copy-start(f32[128,2048]{1,0:T(8,128)} %param.16) | copy-start | bytes 3145732
  11.9 8.4 %collective-permute-start = (bf16[127,2048]{1,0:T(8,128)(2,1)}, bf16[127,2048]{1,0:T(8,128)(2,1)}, u32[]{:S(2)}, u32[]{:S(2)}) collective-permute-start(bf16[127,2048]{1,0:T(8,128)(2,1)} %slice.256), channel_id=1, source_target_pairs={{0,4},{4,8},{8,12},{12,16},{16,20},{20,24},{24,28},{1,5},{5,9},{9,... | collective-permute-start | bytes 1560584 | tf_op jit(solution)/shard_map/ppermute | solution.py:10
  20.3 1.9 copy-start.7
  22.2 45.6 %copy-start.5 = (bf16[512,2048]{1,0:T(8,128)(2,1)S(1)}, bf16[512,2048]{1,0:T(8,128)(2,1)}, u32[]{:S(2)}) copy-start(bf16[512,2048]{1,0:T(8,128)(2,1)} %param.13) | copy-start | bytes 6291460
  67.8 103.6 %copy-start.33 = (f32[2048]{0:T(1024)S(1)}, f32[2048]{0:T(1024)}, u32[]{:S(2)}) copy-start(f32[2048]{0:T(1024)} %param.21) | copy-start | bytes 24580
  67.8 103.6 %copy-start.34 = (f32[2048]{0:T(1024)S(1)}, f32[2048]{0:T(1024)}, u32[]{:S(2)}) copy-start(f32[2048]{0:T(1024)} %param.20) | copy-start | bytes 24580
  70.2 49.7 %collective-permute-start.1 = (bf16[512,2048]{1,0:T(8,128)(2,1)S(1)}, bf16[512,2048]{1,0:T(8,128)(2,1)S(1)}, u32[]{:S(2)}, u32[]{:S(2)}) collective-permute-start(bf16[512,2048]{1,0:T(8,128)(2,1)S(1)} %fusion.4), channel_id=1, source_target_pairs={{0,1},{1,2},{2,3},{3,0},{4,5},{5,6},{6,7},{7,4},{8,9},{9,10},{10,1... | collective-permute-start | bytes 6291464 | tf_op jit(solution)/shard_map/ppermute | solution.py:51
  119.9 1.3 copy-start.1
  121.2 50.2 %collective-permute-start.2 = (bf16[512,2048]{1,0:T(8,128)(2,1)S(1)}, bf16[512,2048]{1,0:T(8,128)(2,1)}, u32[]{:S(2)}, u32[]{:S(2)}) collective-permute-start(bf16[512,2048]{1,0:T(8,128)(2,1)S(1)} %collective-permute-done.1), channel_id=1, source_target_pairs={{0,1},{1,2},{2,3},{3,0},{4,5},{5,6},{6,7},{7,4},{8,9},{9,10},{10,1... | collective-permute-start | bytes 6291464 | tf_op jit(solution)/shard_map/ppermute | solution.py:51
  171.4 49.8 %collective-permute-start.3 = (bf16[512,2048]{1,0:T(8,128)(2,1)}, bf16[512,2048]{1,0:T(8,128)(2,1)}, u32[]{:S(2)}, u32[]{:S(2)}) collective-permute-start(bf16[512,2048]{1,0:T(8,128)(2,1)} %collective-permute-done.2), channel_id=1, source_target_pairs={{0,1},{1,2},{2,3},{3,0},{4,5},{5,6},{6,7},{7,4},{8,9},{9,10},{10,1... | collective-permute-start | bytes 6291464 | tf_op jit(solution)/shard_map/ppermute | solution.py:51
  172.1 112.6 %copy-start.11 = (f32[2048]{0:T(1024)}, f32[2048]{0:T(1024)S(1)}, u32[]{:S(2)}) copy-start(f32[2048]{0:T(1024)S(1)} %get-tuple-element.138) | copy-start | bytes 24580
  172.1 121.2 %copy-start.13 = (f32[2048]{0:T(1024)}, f32[2048]{0:T(1024)S(1)}, u32[]{:S(2)}) copy-start(f32[2048]{0:T(1024)S(1)} %get-tuple-element.141) | copy-start | bytes 24580
  172.1 125.9 %copy-start.15 = (f32[2048]{0:T(1024)}, f32[2048]{0:T(1024)S(1)}, u32[]{:S(2)}) copy-start(f32[2048]{0:T(1024)S(1)} %get-tuple-element.140) | copy-start | bytes 24580
  172.1 131.4 %copy-start.17 = (f32[2048]{0:T(1024)}, f32[2048]{0:T(1024)S(1)}, u32[]{:S(2)}) copy-start(f32[2048]{0:T(1024)S(1)} %get-tuple-element.132) | copy-start | bytes 24580
  172.1 133.8 %copy-start.19 = (f32[2048]{0:T(1024)}, f32[2048]{0:T(1024)S(1)}, u32[]{:S(2)}) copy-start(f32[2048]{0:T(1024)S(1)} %get-tuple-element.133) | copy-start | bytes 24580
  182.8 44.7 %copy-start.2 = (bf16[512,2048]{1,0:T(8,128)(2,1)S(1)}, bf16[512,2048]{1,0:T(8,128)(2,1)}, u32[]{:S(2)}) copy-start(bf16[512,2048]{1,0:T(8,128)(2,1)} %copy-done.1) | copy-start | bytes 6291460
  287.2 38.7 %copy-start = (f32[256,2048]{1,0:T(8,128)}, f32[256,2048]{1,0:T(8,128)S(1)}, u32[]{:S(2)}) copy-start(f32[256,2048]{1,0:T(8,128)S(1)} %multiply_add_fusion) | copy-start | bytes 6291460
  295.0 27.8 %copy-start.3 = (f32[128,2048]{1,0:T(8,128)}, f32[128,2048]{1,0:T(8,128)S(1)}, u32[]{:S(2)}) copy-start(f32[128,2048]{1,0:T(8,128)S(1)} %multiply_add_fusion.1) | copy-start | bytes 3145732
  320.1 17.6 %slice-start.3 = ((f32[8,2048]{1,0:T(8,128)}), f32[1,2048]{1,0:T(1,128)S(1)}, s32[]{:S(2)}) async-start(f32[8,2048]{1,0:T(8,128)} %multiply_add_fusion.5), calls=%async_computation.4 | async-start | bytes 16384 | tf_op jit(solution)/shard_map/slice | solution.py:61
  322.8 14.6 %copy-start.22 = (f32[2048]{0:T(1024)S(1)}, f32[2048]{0:T(1024)}, u32[]{:S(2)}) copy-start(f32[2048]{0:T(1024)} %get-tuple-element.137) | copy-start | bytes 24580
  322.8 14.6 %copy-start.24 = (f32[2,2048]{1,0:T(2,128)S(1)}, f32[2,2048]{1,0:T(2,128)}, u32[]{:S(2)}) copy-start(f32[2,2048]{1,0:T(2,128)} %slice.234) | copy-start | bytes 49156
  322.8 14.6 %copy-start.25 = (f32[2,2048]{1,0:T(2,128)S(1)}, f32[2,2048]{1,0:T(2,128)}, u32[]{:S(2)}) copy-start(f32[2,2048]{1,0:T(2,128)} %slice.235) | copy-start | bytes 49156
  322.8 14.6 %copy-start.29 = (f32[2048]{0:T(1024)S(1)}, f32[2048]{0:T(1024)}, u32[]{:S(2)}) copy-start(f32[2048]{0:T(1024)} %get-tuple-element.136) | copy-start | bytes 24580
  322.8 14.7 %copy-start.9 = (f32[4,2048]{1,0:T(4,128)S(1)}, f32[4,2048]{1,0:T(4,128)}, u32[]{:S(2)}) copy-start(f32[4,2048]{1,0:T(4,128)} %multiply_add_fusion.6) | copy-start | bytes 98308
  322.8 14.8 %copy-start.10 = (f32[3,2048]{1,0:T(4,128)S(1)}, f32[3,2048]{1,0:T(4,128)}, u32[]{:S(2)}) copy-start(f32[3,2048]{1,0:T(4,128)} %slice.242) | copy-start | bytes 73732
  322.8 14.8 %copy-start.23 = (f32[2048]{0:T(1024)S(1)}, f32[2048]{0:T(1024)}, u32[]{:S(2)}) copy-start(f32[2048]{0:T(1024)} %get-tuple-element.134) | copy-start | bytes 24580
  322.9 15.0 %copy-start.8 = (f32[7,2048]{1,0:T(8,128)S(1)}, f32[7,2048]{1,0:T(8,128)}, u32[]{:S(2)}) copy-start(f32[7,2048]{1,0:T(8,128)} %slice.244) | copy-start | bytes 172036
  322.9 15.0 %copy-start.21 = (f32[2048]{0:T(1024)S(1)}, f32[2048]{0:T(1024)}, u32[]{:S(2)}) copy-start(f32[2048]{0:T(1024)} %get-tuple-element.135) | copy-start | bytes 24580
  322.9 15.0 %copy-start.31 = (f32[1,2048]{1,0:T(1,128)S(1)}, f32[1,2048]{1,0:T(1,128)}, u32[]{:S(2)}) copy-start(f32[1,2048]{1,0:T(1,128)} %slice.262) | copy-start | bytes 24580
  322.9 15.1 %copy-start.20 = (f32[2048]{0:T(1024)S(1)}, f32[2048]{0:T(1024)}, u32[]{:S(2)}) copy-start(f32[2048]{0:T(1024)} %copy-done.19) | copy-start | bytes 24580
  325.9 12.2 %copy-start.30 = (f32[1,2048]{1,0:T(1,128)S(1)}, f32[1,2048]{1,0:T(1,128)}, u32[]{:S(2)}) copy-start(f32[1,2048]{1,0:T(1,128)} %slice.261) | copy-start | bytes 24580
  325.9 12.3 %copy-start.18 = (f32[2048]{0:T(1024)S(1)}, f32[2048]{0:T(1024)}, u32[]{:S(2)}) copy-start(f32[2048]{0:T(1024)} %copy-done.17) | copy-start | bytes 24580
  325.9 12.4 %slice-start.2 = ((f32[64,2048]{1,0:T(8,128)}), f32[1,2048]{1,0:T(1,128)S(1)}, s32[]{:S(2)}) async-start(f32[64,2048]{1,0:T(8,128)} %multiply_add_fusion.2), calls=%async_computation.3 | async-start | bytes 16384 | tf_op jit(solution)/shard_map/slice | solution.py:61
  338.0 1.0 copy-start.4
  338.1 1.0 copy-start.16
  338.2 1.0 slice-start.1
  339.1 0.7 copy-start.14
  339.2 2.0 slice-start
  354.6 16.5 %copy-start.12 = (f32[2048]{0:T(1024)S(1)}, f32[2048]{0:T(1024)}, u32[]{:S(2)}) copy-start(f32[2048]{0:T(1024)} %copy-done.11) | copy-start | bytes 24580
  371.1 2.8 copy-start.28
  374.2 24.0 %copy-start.26 = (f32[2048]{0:T(1024)S(1)}, f32[2048]{0:T(1024)}, u32[]{:S(2)}) copy-start(f32[2048]{0:T(1024)} %get-tuple-element.131) | copy-start | bytes 24580
  374.2 24.0 %copy-start.27 = (f32[2048]{0:T(1024)S(1)}, f32[2048]{0:T(1024)}, u32[]{:S(2)}) copy-start(f32[2048]{0:T(1024)} %get-tuple-element.142) | copy-start | bytes 24580
  374.2 24.0 %copy-start.32 = (f32[512]{0:T(512)S(1)}, f32[512]{0:T(512)}, u32[]{:S(2)}) copy-start(f32[512]{0:T(512)} %iota_add_fusion) | copy-start | bytes 6148
Sparse Core Ops, SparseCore 0:
  9.9 163.4 all-gather.3
